TPU v7x, 256 devices: a whole 4x4x8 slice. The times are simulated.
256 devices in a mesh: rows: 256 (over z, y, x, core).
Axes of the slice: x: 4, y: 4, z: 8, core: 2. Of those that a mesh axis runs over, the one named last changes fastest.
Arguments:
- sketch: float32 [524288, 512], P('rows'), may hold values from -100 to 100
- panel: float32 [524288, 512], P('rows'), may hold values from -24 to 24
Outputs:
- basis: float32 [524288, 512], P('rows')
- projected: float32 [512, 512], P('rows')
All inputs are finite; a program needn't handle non-finite values.
Results may differ from a plain program's by a relative error of at most 0.00029.
Values sent between devices are 32-bit elements; how exact they have to be, the bound alone decides.
No kernel may reach another device: no remote copies, remote signals or barrier semaphores. Data moves between devices by JAX's collectives and lax.ppermute only.
A program may use at most 64 MiB of HBM per device.

v0:
```python
import functools

import jax
import jax.numpy as jnp
from jax import lax
from jax.experimental import pallas as pl
from jax.experimental.pallas import tpu as pltpu
from jax.sharding import Mesh, PartitionSpec as P


K = 512
B = 128
G = 8


def dot(a, b, ca, cb, precision=None):
    return lax.dot_general(
        a, b, (((ca,), (cb,)), ((), ())), precision=precision, preferred_element_type=jnp.float32
    )


def halves(x):
    hi = x.astype(jnp.bfloat16)
    return hi, (x - hi.astype(jnp.float32)).astype(jnp.bfloat16)


def dot3(a, b, ca, cb):
    a3 = jnp.concatenate([a[0], a[0], a[1]], axis=ca)
    b3 = jnp.concatenate([b[0], b[1], b[0]], axis=cb)
    return dot(a3, b3, ca, cb)


def thirds(x):
    hi = x.astype(jnp.bfloat16)
    rest = x - hi.astype(jnp.float32)
    mid = rest.astype(jnp.bfloat16)
    return hi, mid, (rest - mid.astype(jnp.float32)).astype(jnp.bfloat16)


def left6(x):
    h, m, l = thirds(x)
    return jnp.concatenate([l, h, m, m, h, h], axis=1)


def right6(x):
    h, m, l = thirds(x)
    return jnp.concatenate([h, l, m, h, m, h], axis=0)


def dot6(a6, b6):
    return dot(a6, b6, 1, 0)


def gram_kernel(core_ref, x_ref, keep_ref, send_ref, acc_ref):
    i = pl.program_id(0)
    h = K // 2
    left = halves(x_ref[:, :h])
    right = halves(x_ref[:, h:])
    parts = (dot3(left, left, 0, 0), dot3(left, right, 0, 0), dot3(right, right, 0, 0))

    @pl.when(i == 0)
    def _():
        for j in range(3):
            acc_ref[j] = parts[j]

    @pl.when(i > 0)
    def _():
        for j in range(3):
            acc_ref[j] += parts[j]

    @pl.when(i == pl.num_programs(0) - 1)
    def _():
        def fold(ref, half):
            if half == 0:
                ref[:, 0:h] = acc_ref[0, 0:B, :]
                ref[:, h:K] = acc_ref[1, 0:B, :]
                ref[:, K:] = acc_ref[2, B:, B:]
            else:
                ref[:, 0:B] = acc_ref[0, B:, B:]
                ref[:, B : 3 * B] = acc_ref[1, B:, :]
                ref[:, 3 * B :] = acc_ref[2, 0:B, :]

        for core in range(2):
            @pl.when(core_ref[0] == core)
            def _():
                fold(keep_ref, core)
                fold(send_ref, 1 - core)


def folded_gram(core, sketch, tile=1024):
    rows = sketch.shape[0]
    out = jax.ShapeDtypeStruct((B, K + B), jnp.float32)
    whole = pl.BlockSpec((B, K + B), lambda i: (0, 0))
    return pl.pallas_call(
        gram_kernel,
        out_shape=(out, out),
        grid=(rows // tile,),
        in_specs=[
            pl.BlockSpec(memory_space=pltpu.SMEM),
            pl.BlockSpec((tile, K), lambda i: (i, 0)),
        ],
        out_specs=(whole, whole),
        scratch_shapes=[pltpu.VMEM((3, K // 2, K // 2), jnp.float32)],
        cost_estimate=pl.CostEstimate(
            flops=6 * rows * K * K, bytes_accessed=4 * rows * K, transcendentals=0
        ),
        compiler_params=pltpu.CompilerParams(vmem_limit_bytes=24 << 20),
        name="gram",
    )(core, sketch)


def cross_kernel(p_ref, x_ref, o_ref):
    x = halves(x_ref[...])
    p = halves(p_ref[...])
    part = dot3(p, x, 0, 0)

    @pl.when(pl.program_id(0) == 0)
    def _():
        o_ref[...] = part

    @pl.when(pl.program_id(0) > 0)
    def _():
        o_ref[...] += part


def cross_product(panel, sketch, tile=1024):
    rows, frames = panel.shape
    return pl.pallas_call(
        cross_kernel,
        out_shape=jax.ShapeDtypeStruct((frames, K), jnp.float32),
        grid=(rows // tile,),
        in_specs=[
            pl.BlockSpec((tile, frames), lambda i: (i, 0)),
            pl.BlockSpec((tile, K), lambda i: (i, 0)),
        ],
        out_specs=pl.BlockSpec((frames, K), lambda i: (0, 0)),
        cost_estimate=pl.CostEstimate(
            flops=6 * rows * K * frames, bytes_accessed=8 * rows * K, transcendentals=0
        ),
        compiler_params=pltpu.CompilerParams(vmem_limit_bytes=28 << 20),
        name="cross",
    )(panel, sketch)


def factor_block(t, bc_ref):
    n = B // G
    lane = lax.broadcasted_iota(jnp.int32, (G, B), 1)
    sub = lax.broadcasted_iota(jnp.int32, (G, B), 0)
    out = []
    for s in range(n):
        c0 = s * G
        tj = t[s]
        ahead = s + 1 < n

        def lanes_of(v, b):
            return jnp.broadcast_to(v[:, c0 + b : c0 + b + 1], (G, B))

        inside = (lane >= c0) & (lane < c0 + G)
        m = []
        for b in range(G):
            bc_ref[s, b] = lanes_of(tj, b)
            if ahead:
                m.append(lanes_of(t[s + 1], b))
        bc_ref[s, G] = jnp.where(inside, jnp.where(lane - c0 == sub, 1.0, 0.0), tj)
        p = [[None] * G for _ in range(G)]
        for b in range(G):
            for a in range(b + 1):
                p[a][b] = bc_ref[s, b, pl.ds(a, G, stride=0), :]
        r = [bc_ref[s, G, pl.ds(a, G, stride=0), :] for a in range(G)]
        if ahead:
            acc = jnp.where(inside, 0.0, t[s + 1])
        dinv = [None] * G
        for b in range(G):
            d = 1.0 / p[b][b]
            dinv[b] = d
            if b + 1 < G:
                p[b + 1][b + 1] = p[b + 1][b + 1] - (p[b][b + 1] * p[b][b + 1]) * d
            for a in range(b + 1, G):
                w = p[b][a] * d
                for c in range(a, G):
                    if (a, c) != (b + 1, b + 1):
                        p[a][c] = p[a][c] - w * p[b][c]
                r[a] = r[a] - w * r[b]
            if ahead:
                u = m[b] * d
                for c in range(b + 1, G):
                    m[c] = m[c] - u * p[b][c]
                acc = acc - u * r[b]
        if ahead:
            y = [None] * G
            for b in range(G - 1, -1, -1):
                v = r[b] * dinv[b]
                for c in range(b + 1, G):
                    v = v - (p[b][c] * dinv[b]) * y[c]
                y[b] = v
            rest = [jnp.where(inside, 0.0, t[g]) for g in range(s + 2, n)]
            for b in range(G - 1, -1, -1):
                for i, g in enumerate(range(s + 2, n)):
                    rest[i] = rest[i] - lanes_of(t[g], b) * y[b]
            t[s + 1] = acc
            t[s + 2 :] = rest
        rs = [r[a] * lax.rsqrt(p[a][a]) for a in range(G)]
        o = rs[G - 1]
        for a in range(G - 2, -1, -1):
            o = jnp.where(sub == a, rs[a], o)
        out.append(jnp.where(lane <= sub + c0, o, 0.0))
    return out


def factor_kernel(core_ref, mine_ref, other_ref, w_ref, fold_ref, s_ref, bc_ref):
    core = core_ref[0]
    fold_ref[core] = mine_ref[...]
    fold_ref[1 - core] = other_ref[...]
    nb = K // B
    s_ref[0:B, :] = fold_ref[0, :, 0:K]
    s_ref[3 * B : 4 * B, 3 * B :] = fold_ref[0, :, K:]
    s_ref[B : 2 * B, B:] = fold_ref[1, :, 0 : 3 * B]
    s_ref[2 * B : 3 * B, 2 * B :] = fold_ref[1, :, 3 * B :]
    for i in range(1, nb):
        s_ref[i * B : (i + 1) * B, : i * B] = jnp.zeros((B, i * B), jnp.float32)
    for k in range(nb):
        k0, k1, k2 = k * B, (k + 1) * B, (k + 2) * B
        last = k + 1 == nb
        t = [s_ref[k0 + g * G : k0 + (g + 1) * G, k0:k1] for g in range(B // G)]
        for g, rows in enumerate(factor_block(t, bc_ref)):
            w_ref[k0 + g * G : k0 + (g + 1) * G, k0:k1] = rows
        linv = w_ref[k0:k1, k0:k1]
        linv6 = left6(linv)
        if not last:
            w_ref[k0:k1, k1:] = jnp.zeros((B, K - k1), jnp.float32)
            near = dot6(linv6, right6(s_ref[k0:k1, k1:k2]))
            near6 = left6(near.T)
            s_ref[k1:k2, k1:k2] = s_ref[k1:k2, k1:k2] - dot6(near6, right6(near))
        if k:
            left = dot6(linv6, right6(s_ref[k0:k1, :k0]))
            w_ref[k0:k1, :k0] = left
        if not last:
            done = [left, linv] if k else [linv]
            done6 = right6(jnp.concatenate(done, axis=1))
            if k + 2 < nb:
                far = dot6(linv6, right6(s_ref[k0:k1, k2:]))
                far6 = right6(far)
            for i in range(k + 1, nb):
                i0, i1 = i * B, (i + 1) * B
                if i == k + 1:
                    lt6 = near6
                else:
                    f0 = (i - k - 2) * B
                    lt6 = left6(far[:, f0 : f0 + B].T)
                s_ref[i0:i1, :k1] = s_ref[i0:i1, :k1] - dot6(lt6, done6)
                if k + 2 < nb:
                    j0 = max(i, k + 2) * B
                    s_ref[i0:i1, j0:] = s_ref[i0:i1, j0:] - dot6(lt6, far6[:, j0 - k2 :])


def lower_inverse(core, mine, other):
    vmem = pl.BlockSpec(memory_space=pltpu.VMEM)
    return pl.pallas_call(
        factor_kernel,
        out_shape=jax.ShapeDtypeStruct((K, K), jnp.float32),
        in_specs=[pl.BlockSpec(memory_space=pltpu.SMEM), vmem, vmem],
        out_specs=vmem,
        scratch_shapes=[
            pltpu.VMEM((2, B, K + B), jnp.float32),
            pltpu.VMEM((K, K), jnp.float32),
            pltpu.VMEM((B // G, G + 1, G, B), jnp.float32),
        ],
        cost_estimate=pl.CostEstimate(flops=8_000_000_000, bytes_accessed=2_000_000, transcendentals=0),
        compiler_params=pltpu.CompilerParams(vmem_limit_bytes=12 << 20),
        name="factor",
    )(core, mine, other)


def basis_kernel(scale, x_ref, w_ref, c_ref, o_ref, q_ref, hi_ref, lo_ref):
    h = K // 2

    def times(rows):
        rl, rr = halves(rows[:, :h]), halves(rows[:, h:])
        wl = (hi_ref[:h, :h], lo_ref[:h, :h])
        wr = (hi_ref[h:, :h], lo_ref[h:, :h]), (hi_ref[h:, h:], lo_ref[h:, h:])
        return dot3(rl, wl, 1, 1), dot3(rl, wr[0], 1, 1) + dot3(rr, wr[1], 1, 1)

    @pl.when(pl.program_id(0) == 0)
    def _():
        hi_ref[...], lo_ref[...] = halves(w_ref[...])
        left, right = times(c_ref[...])
        q_ref[:, :h] = left * scale
        q_ref[:, h:] = right * scale

    o_ref[:, :h], o_ref[:, h:] = times(x_ref[...])


def apply_inverse(sketch, winv, crows, scale, tile=1024):
    rows = sketch.shape[0]
    n = crows.shape[0]
    fixed = pl.BlockSpec((K, K), lambda i: (0, 0))
    small = pl.BlockSpec((n, K), lambda i: (0, 0))
    return pl.pallas_call(
        functools.partial(basis_kernel, scale),
        out_shape=(
            jax.ShapeDtypeStruct((rows, K), jnp.float32),
            jax.ShapeDtypeStruct((n, K), jnp.float32),
        ),
        grid=(rows // tile,),
        in_specs=[pl.BlockSpec((tile, K), lambda i: (i, 0)), fixed, small],
        out_specs=(pl.BlockSpec((tile, K), lambda i: (i, 0)), small),
        scratch_shapes=[pltpu.VMEM((K, K), jnp.bfloat16)] * 2,
        cost_estimate=pl.CostEstimate(
            flops=6 * rows * K * K, bytes_accessed=8 * rows * K, transcendentals=0
        ),
        compiler_params=pltpu.CompilerParams(vmem_limit_bytes=24 << 20),
        name="basis",
    )(sketch, winv, crows)


PLANE = ("y", "x")
SWAP = [(0, 1), (1, 0)]


def shift(x, by, n):
    return lax.ppermute(x, "z", [(i, (i + by) % n) for i in range(n)])


def sum_over_ring(x):
    n = lax.axis_size("z")
    before = shift(x, 1, n)
    after = shift(x, -1, n)
    two = x + before
    three = two + after
    return three + shift(three, 3, n) + shift(two, -3, n)


def on_device(sketch, panel):
    core = lax.axis_index("c").astype(jnp.int32)
    plane = lax.axis_size(PLANE)
    ring = lax.axis_size("z")
    rows_all = sketch.shape[0] * plane * ring * 2

    keep, send = folded_gram(core.reshape(1), sketch)
    half = keep + lax.ppermute(send, "c", SWAP)
    got = lax.all_to_all(half.reshape(plane, B // plane, K + B), PLANE, 0, 0, tiled=True)
    part = sum_over_ring(jnp.sum(got, axis=0)) * (1.0 / rows_all)
    mine = lax.all_to_all(
        jnp.broadcast_to(part, (plane,) + part.shape), PLANE, 0, 0, tiled=True
    ).reshape(B, K + B)
    other = lax.ppermute(mine, "c", SWAP)
    winv = lower_inverse(core.reshape(1), mine, other)

    cross = cross_product(panel, sketch)
    frames = cross.shape[0] // (ring * plane * 2)
    cross = cross.reshape(ring, plane, 2, frames, K)
    ckeep = lax.dynamic_index_in_dim(cross, core, 2, keepdims=False)
    csend = lax.dynamic_index_in_dim(cross, 1 - core, 2, keepdims=False)
    chalf = ckeep + lax.ppermute(csend, "c", SWAP)
    chalf = chalf.transpose(1, 0, 2, 3).reshape(plane, ring * frames, K)
    got = lax.all_to_all(chalf, PLANE, 0, 0, tiled=True)
    crows = jnp.sum(got, axis=0).reshape(ring, frames, K)
    got = lax.all_to_all(crows, "z", 0, 0, tiled=True)
    crows = jnp.sum(got, axis=0)

    return apply_inverse(sketch, winv, crows, rows_all ** -0.5)


def solution(mesh):
    torus = Mesh(mesh.devices.reshape(8, 4, 4, 2), ("z", "y", "x", "c"))
    spec = P(("z", "y", "x", "c"), None)

    return jax.shard_map(
        on_device,
        mesh=torus,
        in_specs=(spec, spec),
        out_specs=(spec, spec),
        check_vma=False,
    )
```

profile of v0, /device:TPU:2, one launch (start us, length us, event | category | flops | bytes accessed | tf_op | source)
XLA Modules:
  0.0 102.2 jit_solution(10975772591582885800)
XLA Ops:
  0.6 2.2 %copy-done.1 = f32[2048,512]{1,0:T(8,128)S(1)} copy-done((f32[2048,512]{1,0:T(8,128)S(1)}, f32[2048,512]{1,0:T(8,128)}, u32[]{:S(2)}) %copy-start.1) | copy-done | bytes 4194328
  2.8 3.1 %gram.1 = (f32[128,640]{1,0:T(8,128)S(1)}, f32[128,640]{1,0:T(8,128)S(1)}) custom-call(s32[1]{0:T(128)} %bitcast.core_ref, f32[2048,512]{1,0:T(8,128)S(1)} %copy-done.1), custom_call_target="tpu_custom_call" | custom-call | flops 3221225472 | bytes 4194304 | tf_op jit(solution)/shard_map/gram/pallas_call | solution.py:94
  6.1 1.6 %collective-permute-done = f32[128,640]{1,0:T(8,128)S(1)} collective-permute-done((f32[128,640]{1,0:T(8,128)S(1)}, f32[128,640]{1,0:T(8,128)S(1)}, u32[]{:S(2)}, u32[]{:S(2)}) %collective-permute-start) | collective-permute-done | bytes 327712 | tf_op jit(solution)/shard_map/ppermute | solution.py:340
  7.7 0.8 add_bitcast_fusion
  8.4 7.5 %all-to-all-start = ((f32[16,8,640]{2,1,0:T(8,128)}), f32[16,8,640]{2,1,0:T(8,128)S(1)}, u32[]{:S(2)}, u32[]{:S(2)}) async-start(f32[16,8,640]{2,1,0:T(8,128)} %add_bitcast_fusion), calls=%async_computation | async-start | bytes 655360 | tf_op jit(solution)/shard_map/all_to_all | solution.py:341
  15.9 2.2 %copy-done = f32[2048,512]{1,0:T(8,128)S(1)} copy-done((f32[2048,512]{1,0:T(8,128)S(1)}, f32[2048,512]{1,0:T(8,128)}, u32[]{:S(2)}) %copy-start) | copy-done | bytes 4194328
  18.1 2.2 %copy-done.2 = f32[2048,512]{1,0:T(8,128)S(1)} copy-done((f32[2048,512]{1,0:T(8,128)S(1)}, f32[2048,512]{1,0:T(8,128)}, u32[]{:S(2)}) %copy-start.2) | copy-done | bytes 4194328
  20.3 3.8 %cross.1 = f32[512,512]{1,0:T(8,128)S(1)} custom-call(f32[2048,512]{1,0:T(8,128)S(1)} %copy-done, f32[2048,512]{1,0:T(8,128)S(1)} %copy-done.2), custom_call_target="tpu_custom_call" | custom-call | flops 3221225472 | bytes 8388608 | tf_op jit(solution)/shard_map/cross/pallas_call | solution.py:128
  24.8 5.9 %collective-permute-start.2 = (f32[8,640]{1,0:T(8,128)S(1)}, f32[8,640]{1,0:T(8,128)S(1)}, u32[]{:S(2)}, u32[]{:S(2)}) collective-permute-start(f32[8,640]{1,0:T(8,128)S(1)} %reduce_sum.27), channel_id=1, source_target_pairs={{0,224},{32,0},{64,32},{96,64},{128,96},{160,128},{192,160},{224,1... | collective-permute-start | bytes 61448 | tf_op jit(solution)/shard_map/ppermute | solution.py:321
  31.3 0.9 collective-permute-done.2
  32.2 3.5 %collective-permute-done.1 = f32[8,640]{1,0:T(8,128)S(1)} collective-permute-done((f32[8,640]{1,0:T(8,128)S(1)}, f32[8,640]{1,0:T(8,128)S(1)}, u32[]{:S(2)}, u32[]{:S(2)}) %collective-permute-start.1) | collective-permute-done | bytes 20512 | tf_op jit(solution)/shard_map/ppermute | solution.py:321
  35.7 0.7 collective-permute-start.4
  36.4 3.1 %collective-permute-start.3 = (f32[8,640]{1,0:T(8,128)S(1)}, f32[8,640]{1,0:T(8,128)S(1)}, u32[]{:S(2)}, u32[]{:S(2)}) collective-permute-start(f32[8,640]{1,0:T(8,128)S(1)} %get-tuple-element.6), channel_id=1, source_target_pairs={{0,96},{32,128},{64,160},{96,192},{128,224},{160,0},{192,32},{224,... | collective-permute-start | bytes 61448 | tf_op jit(solution)/shard_map/ppermute | solution.py:321
  39.6 1.8 %collective-permute-done.4 = f32[8,640]{1,0:T(8,128)S(1)} collective-permute-done((f32[8,640]{1,0:T(8,128)S(1)}, f32[8,640]{1,0:T(8,128)S(1)}, u32[]{:S(2)}, u32[]{:S(2)}) %collective-permute-start.4) | collective-permute-done | bytes 20512 | tf_op jit(solution)/shard_map/ppermute | solution.py:321
  41.3 1.9 %collective-permute-done.3 = f32[8,640]{1,0:T(8,128)S(1)} collective-permute-done((f32[8,640]{1,0:T(8,128)S(1)}, f32[8,640]{1,0:T(8,128)S(1)}, u32[]{:S(2)}, u32[]{:S(2)}) %collective-permute-start.3) | collective-permute-done | bytes 20512 | tf_op jit(solution)/shard_map/ppermute | solution.py:321
  43.2 0.7 broadcast_in_dim.3
  44.0 7.2 %all-to-all-start.1 = ((f32[16,8,640]{2,1,0:T(8,128)}), f32[16,8,640]{2,1,0:T(8,128)S(1)}, u32[]{:S(2)}, u32[]{:S(2)}) async-start(f32[16,8,640]{2,1,0:T(8,128)} %broadcast_in_dim.3), calls=%async_computation.1 | async-start | bytes 655360 | tf_op jit(solution)/shard_map/all_to_all | solution.py:343
  51.3 1.1 %copy.14 = f32[16,16,512]{2,1,0:T(8,128)} copy(f32[16,16,512]{2,0,1:T(8,128)S(1)} %bitcast.14) | data formatting | bytes 1048576 | tf_op jit(solution)/shard_map/reshape | solution.py:355
  52.4 6.4 %all-to-all-done.1 = f32[16,8,640]{2,1,0:T(8,128)S(1)} async-done(((f32[16,8,640]{2,1,0:T(8,128)}), f32[16,8,640]{2,1,0:T(8,128)S(1)}, u32[]{:S(2)}, u32[]{:S(2)}) %all-to-all-start.1) | async-done | bytes 327712 | tf_op jit(solution)/shard_map/all_to_all | solution.py:343
  58.9 4.8 %all-to-all-start.2 = ((f32[16,16,512]{2,1,0:T(8,128)}), f32[16,16,512]{2,1,0:T(8,128)S(1)}, u32[]{:S(2)}, u32[]{:S(2)}) async-start(f32[16,16,512]{2,1,0:T(8,128)} %copy.14), calls=%async_computation.2 | async-start | bytes 1048576 | tf_op jit(solution)/shard_map/all_to_all | solution.py:356
  63.7 8.9 %all-to-all-done.2 = f32[16,16,512]{2,1,0:T(8,128)S(1)} async-done(((f32[16,16,512]{2,1,0:T(8,128)}), f32[16,16,512]{2,1,0:T(8,128)S(1)}, u32[]{:S(2)}, u32[]{:S(2)}) %all-to-all-start.2) | async-done | bytes 524320 | tf_op jit(solution)/shard_map/all_to_all | solution.py:356
  72.6 11.7 %all_to_all.20 = f32[8,2,512]{2,1,0:T(2,128)S(1)} all-to-all(f32[8,2,512]{2,1,0:T(2,128)S(1)} %reshape.28), channel_id=1, replica_groups=mesh['z'=8,'y'=4,'x'=4,'c'=2] {'z'}, dimensions={0} | all-to-all | bytes 65536 | tf_op jit(solution)/shard_map/all_to_all | solution.py:358
  84.4 13.1 %factor.1.w_ref = f32[512,512]{1,0:T(8,128)S(1)} custom-call(s32[1]{0:T(128)} %bitcast.core_ref, f32[128,640]{1,0:T(8,128)S(1)} %bitcast.13, f32[128,640]{1,0:T(8,128)S(1)} %collective-permute-done.5.other_ref), custom_call_target="tpu_custom_call" | custom-call | flops 8000000000 | bytes 2000000 | tf_op jit(solution)/shard_map/factor/pallas_call | solution.py:258
  97.4 4.7 %basis.1 = (f32[2048,512]{1,0:T(8,128)}, f32[2,512]{1,0:T(2,128)}) custom-call(f32[2048,512]{1,0:T(8,128)S(1)} %copy-done.3, f32[512,512]{1,0:T(8,128)S(1)} %factor.1.w_ref, f32[2,512]{1,0:T(2,128)S(1)} %reduce_sum.29.c_ref), custom_call_target="tpu_custom_call" | custom-call | flops 3221225472 | bytes 8388608 | tf_op jit(solution)/shard_map/basis/pallas_call | solution.py:298
  (22 shorter events, 1.5 us)
Async XLA Ops:
  0.6 2.2 %copy-start.1 = (f32[2048,512]{1,0:T(8,128)S(1)}, f32[2048,512]{1,0:T(8,128)}, u32[]{:S(2)}) copy-start(f32[2048,512]{1,0:T(8,128)} %x_ref.5) | copy-start | bytes 12582916
  6.0 1.7 %collective-permute-start = (f32[128,640]{1,0:T(8,128)S(1)}, f32[128,640]{1,0:T(8,128)S(1)}, u32[]{:S(2)}, u32[]{:S(2)}) collective-permute-start(f32[128,640]{1,0:T(8,128)S(1)} %get-tuple-element.5), channel_id=1, source_target_pairs={{0,1},{1,0},{2,3},{3,2},{4,5},{5,4},{6,7},{7,6},{8,9},{9,8},{10,11... | collective-permute-start | bytes 983048 | tf_op jit(solution)/shard_map/ppermute | solution.py:340
  8.4 16.3 %all-to-all-start = ((f32[16,8,640]{2,1,0:T(8,128)}), f32[16,8,640]{2,1,0:T(8,128)S(1)}, u32[]{:S(2)}, u32[]{:S(2)}) async-start(f32[16,8,640]{2,1,0:T(8,128)} %add_bitcast_fusion), calls=%async_computation | async-start | bytes 655360 | tf_op jit(solution)/shard_map/all_to_all | solution.py:341
  15.9 2.2 %copy-start = (f32[2048,512]{1,0:T(8,128)S(1)}, f32[2048,512]{1,0:T(8,128)}, u32[]{:S(2)}) copy-start(f32[2048,512]{1,0:T(8,128)} %p_ref.1) | copy-start | bytes 12582916
  18.1 2.2 %copy-start.2 = (f32[2048,512]{1,0:T(8,128)S(1)}, f32[2048,512]{1,0:T(8,128)}, u32[]{:S(2)}) copy-start(f32[2048,512]{1,0:T(8,128)} %x_ref.5) | copy-start | bytes 12582916
  24.8 7.4 %collective-permute-start.2 = (f32[8,640]{1,0:T(8,128)S(1)}, f32[8,640]{1,0:T(8,128)S(1)}, u32[]{:S(2)}, u32[]{:S(2)}) collective-permute-start(f32[8,640]{1,0:T(8,128)S(1)} %reduce_sum.27), channel_id=1, source_target_pairs={{0,224},{32,0},{64,32},{96,64},{128,96},{160,128},{192,160},{224,1... | collective-permute-start | bytes 61448 | tf_op jit(solution)/shard_map/ppermute | solution.py:321
  30.7 5.0 %collective-permute-start.1 = (f32[8,640]{1,0:T(8,128)S(1)}, f32[8,640]{1,0:T(8,128)S(1)}, u32[]{:S(2)}, u32[]{:S(2)}) collective-permute-start(f32[8,640]{1,0:T(8,128)S(1)} %reduce_sum.27), channel_id=1, source_target_pairs={{0,32},{32,64},{64,96},{96,128},{128,160},{160,192},{192,224},{224... | collective-permute-start | bytes 61448 | tf_op jit(solution)/shard_map/ppermute | solution.py:321
  31.2 20.0 %collective-permute-start.6 = (f32[8,16,2,512]{3,1,2,0:T(8,128)S(1)}, f32[8,16,2,512]{3,1,2,0:T(8,128)S(1)}, u32[]{:S(2)}, u32[]{:S(2)}) collective-permute-start(f32[8,16,2,512]{3,1,2,0:T(8,128)S(1)} %bitcast.15), channel_id=1, source_target_pairs={{0,1},{1,0},{2,3},{3,2},{4,5},{5,4},{6,7},{7,6},{8,9},{9,8},{10,11... | collective-permute-start | bytes 1572872 | tf_op jit(solution)/shard_map/ppermute | solution.py:354
  35.7 5.6 %collective-permute-start.4 = (f32[8,640]{1,0:T(8,128)S(1)}, f32[8,640]{1,0:T(8,128)S(1)}, u32[]{:S(2)}, u32[]{:S(2)}) collective-permute-start(f32[8,640]{1,0:T(8,128)S(1)} %get-tuple-element.7), channel_id=1, source_target_pairs={{0,160},{32,192},{64,224},{96,0},{128,32},{160,64},{192,96},{224,1... | collective-permute-start | bytes 61448 | tf_op jit(solution)/shard_map/ppermute | solution.py:321
  36.4 6.8 %collective-permute-start.3 = (f32[8,640]{1,0:T(8,128)S(1)}, f32[8,640]{1,0:T(8,128)S(1)}, u32[]{:S(2)}, u32[]{:S(2)}) collective-permute-start(f32[8,640]{1,0:T(8,128)S(1)} %get-tuple-element.6), channel_id=1, source_target_pairs={{0,96},{32,128},{64,160},{96,192},{128,224},{160,0},{192,32},{224,... | collective-permute-start | bytes 61448 | tf_op jit(solution)/shard_map/ppermute | solution.py:321
  44.0 14.9 %all-to-all-start.1 = ((f32[16,8,640]{2,1,0:T(8,128)}), f32[16,8,640]{2,1,0:T(8,128)S(1)}, u32[]{:S(2)}, u32[]{:S(2)}) async-start(f32[16,8,640]{2,1,0:T(8,128)} %broadcast_in_dim.3), calls=%async_computation.1 | async-start | bytes 655360 | tf_op jit(solution)/shard_map/all_to_all | solution.py:343
  58.9 13.7 %all-to-all-start.2 = ((f32[16,16,512]{2,1,0:T(8,128)}), f32[16,16,512]{2,1,0:T(8,128)S(1)}, u32[]{:S(2)}, u32[]{:S(2)}) async-start(f32[16,16,512]{2,1,0:T(8,128)} %copy.14), calls=%async_computation.2 | async-start | bytes 1048576 | tf_op jit(solution)/shard_map/all_to_all | solution.py:356
  63.7 20.7 %collective-permute-start.5 = (f32[128,640]{1,0:T(8,128)S(1)}, f32[128,640]{1,0:T(8,128)S(1)}, u32[]{:S(2)}, u32[]{:S(2)}) collective-permute-start(f32[128,640]{1,0:T(8,128)S(1)} %bitcast.12), channel_id=1, source_target_pairs={{0,1},{1,0},{2,3},{3,2},{4,5},{5,4},{6,7},{7,6},{8,9},{9,8},{10,11... | collective-permute-start | bytes 983048 | tf_op jit(solution)/shard_map/ppermute | solution.py:346
  84.3 13.1 %copy-start.3 = (f32[2048,512]{1,0:T(8,128)S(1)}, f32[2048,512]{1,0:T(8,128)}, u32[]{:S(2)}) copy-start(f32[2048,512]{1,0:T(8,128)} %x_ref.5) | copy-start | bytes 12582916
where the time goes:
time: 103 us; the launch traced here: 102 us
  starting transfers between devices  29.5 us (29%)
  waiting for transfers between devices  25 us (24%)
  Pallas kernels  24.7 us (24%)
  blocking collectives  11.7 us (11%)
  local copies, waits for them, and re-layouts  9.51 us (9%)
    pallas_call x1, Pallas kernels, lower_inverse(): pl.pallas_call(factor_kernel, out_shape=jax.ShapeDtypeStruct((K, K), jnp....  13.1 us
    all_to_all x1, blocking collectives, on_device(): got = lax.all_to_all(crows, 'z', 0, 0, tiled=True)  11.7 us
    ppermute x4, starting transfers between devices, shift(): return lax.ppermute(x, 'z', [(i, (i + by) % n) for i in range(n)])  9.77 us
    all_to_all x1, waiting for transfers between devices, on_device(): got = lax.all_to_all(chalf, PLANE, 0, 0, tiled=True)  8.86 us
    ppermute x4, waiting for transfers between devices, shift(): return lax.ppermute(x, 'z', [(i, (i + by) % n) for i in range(n)])  8.07 us
    all_to_all x1, starting transfers between devices, on_device(): lax.all_to_all(half.reshape(plane, B // plane, K + B), PLANE, 0, 0, tiled...  7.48 us
    all_to_all x1, starting transfers between devices, on_device(): lax.all_to_all(jnp.broadcast_to(part, (plane,) + part.shape), PLANE, 0, 0...  7.23 us
    unnamed x8, local copies, waits for them, and re-layouts  6.56 us
  transfers between devices with their start and end apart: 10, of which 7 were waited for; matrix products, arithmetic and copies ran while one was open for 3% of the time, Pallas kernels for 4%

commit v1 on v0

--- a/solution.py
+++ b/solution.py
@@ -51,95 +51,126 @@
     return dot(a6, b6, 1, 0)
 
 
-def gram_kernel(core_ref, x_ref, keep_ref, send_ref, acc_ref):
-    i = pl.program_id(0)
+VMEM = pl.BlockSpec(memory_space=pltpu.VMEM)
+SMEM = pl.BlockSpec(memory_space=pltpu.SMEM)
+HBM = pl.BlockSpec(memory_space=pltpu.HBM)
+
+
+def start_loads(pairs, sems, sizes):
+    loads, start = [], 0
+    for i, size in enumerate(sizes):
+        at = pl.ds(start, size)
+        loads.append(
+            [pltpu.make_async_copy(src.at[at], dst.at[at], sems.at[j, i]) for j, (src, dst) in enumerate(pairs)]
+        )
+        for load in loads[-1]:
+            load.start()
+        start += size
+    return loads
+
+
+GRAM_STEPS = (256, 256, 512, 512, 512)
+CROSS_STEPS = (256, 256, 512, 1024)
+BASIS_STEPS = (256, 256, 512, 512, 256, 256)
+
+
+def gram_kernel(core_ref, x_hbm, keep_ref, send_ref, x_ref, acc_ref, sems):
+    loads = start_loads(((x_hbm, x_ref),), sems, GRAM_STEPS)
     h = K // 2
-    left = halves(x_ref[:, :h])
-    right = halves(x_ref[:, h:])
-    parts = (dot3(left, left, 0, 0), dot3(left, right, 0, 0), dot3(right, right, 0, 0))
-
-    @pl.when(i == 0)
-    def _():
+    start = 0
+    for i, size in enumerate(GRAM_STEPS):
+        loads[i][0].wait()
+        rows = slice(start, start + size)
+        start += size
+        left = halves(x_ref[rows, :h])
+        right = halves(x_ref[rows, h:])
+        parts = (dot3(left, left, 0, 0), dot3(left, right, 0, 0), dot3(right, right, 0, 0))
         for j in range(3):
-            acc_ref[j] = parts[j]
-
-    @pl.when(i > 0)
-    def _():
-        for j in range(3):
-            acc_ref[j] += parts[j]
-
-    @pl.when(i == pl.num_programs(0) - 1)
-    def _():
-        def fold(ref, half):
-            if half == 0:
-                ref[:, 0:h] = acc_ref[0, 0:B, :]
-                ref[:, h:K] = acc_ref[1, 0:B, :]
-                ref[:, K:] = acc_ref[2, B:, B:]
-            else:
-                ref[:, 0:B] = acc_ref[0, B:, B:]
-                ref[:, B : 3 * B] = acc_ref[1, B:, :]
-                ref[:, 3 * B :] = acc_ref[2, 0:B, :]
-
-        for core in range(2):
-            @pl.when(core_ref[0] == core)
-            def _():
-                fold(keep_ref, core)
-                fold(send_ref, 1 - core)
-
-
-def folded_gram(core, sketch, tile=1024):
+            acc_ref[j] = parts[j] if i == 0 else acc_ref[j] + parts[j]
+
+    def fold(ref, half):
+        if half == 0:
+            ref[:, 0:h] = acc_ref[0, 0:B, :]
+            ref[:, h:K] = acc_ref[1, 0:B, :]
+            ref[:, K:] = acc_ref[2, B:, B:]
+        else:
+            ref[:, 0:B] = acc_ref[0, B:, B:]
+            ref[:, B : 3 * B] = acc_ref[1, B:, :]
+            ref[:, 3 * B :] = acc_ref[2, 0:B, :]
+
+    for core in range(2):
+        @pl.when(core_ref[0] == core)
+        def _():
+            fold(keep_ref, core)
+            fold(send_ref, 1 - core)
+
+
+def folded_gram(core, sketch):
     rows = sketch.shape[0]
-    out = jax.ShapeDtypeStruct((B, K + B), jnp.float32)
-    whole = pl.BlockSpec((B, K + B), lambda i: (0, 0))
+    half = jax.ShapeDtypeStruct((B, K + B), jnp.float32)
     return pl.pallas_call(
         gram_kernel,
-        out_shape=(out, out),
-        grid=(rows // tile,),
-        in_specs=[
-            pl.BlockSpec(memory_space=pltpu.SMEM),
-            pl.BlockSpec((tile, K), lambda i: (i, 0)),
+        out_shape=(half, half),
+        in_specs=[SMEM, HBM],
+        out_specs=(VMEM, VMEM),
+        scratch_shapes=[
+            pltpu.VMEM(sketch.shape, jnp.float32),
+            pltpu.VMEM((3, K // 2, K // 2), jnp.float32),
+            pltpu.SemaphoreType.DMA((1, len(GRAM_STEPS))),
         ],
-        out_specs=(whole, whole),
-        scratch_shapes=[pltpu.VMEM((3, K // 2, K // 2), jnp.float32)],
         cost_estimate=pl.CostEstimate(
             flops=6 * rows * K * K, bytes_accessed=4 * rows * K, transcendentals=0
         ),
-        compiler_params=pltpu.CompilerParams(vmem_limit_bytes=24 << 20),
+        compiler_params=pltpu.CompilerParams(vmem_limit_bytes=52 << 20),
         name="gram",
     )(core, sketch)
 
 
-def cross_kernel(p_ref, x_ref, o_ref):
-    x = halves(x_ref[...])
-    p = halves(p_ref[...])
-    part = dot3(p, x, 0, 0)
-
-    @pl.when(pl.program_id(0) == 0)
-    def _():
-        o_ref[...] = part
-
-    @pl.when(pl.program_id(0) > 0)
-    def _():
-        o_ref[...] += part
-
-
-def cross_product(panel, sketch, tile=1024):
+def cross_kernel(core_ref, p_hbm, x_hbm, keep_ref, send_ref, p_ref, x_ref, acc_ref, sems):
+    loads = start_loads(((p_hbm, p_ref), (x_hbm, x_ref)), sems, CROSS_STEPS)
+    start = 0
+    for i, size in enumerate(CROSS_STEPS):
+        for load in loads[i]:
+            load.wait()
+        rows = slice(start, start + size)
+        start += size
+        part = dot3(halves(p_ref[rows, :]), halves(x_ref[rows, :]), 0, 0)
+        acc_ref[...] = part if i == 0 else acc_ref[...] + part
+    plane, ring = keep_ref.shape[0], keep_ref.shape[1] // 2
+
+    def pack(ref, core):
+        for z in range(ring):
+            for d in range(plane):
+                f = (z * plane + d) * 4 + core * 2
+                ref[d, 2 * z : 2 * z + 2, :] = acc_ref[f : f + 2, :]
+
+    for core in range(2):
+        @pl.when(core_ref[0] == core)
+        def _():
+            pack(keep_ref, core)
+            pack(send_ref, 1 - core)
+
+
+def cross_product(core, panel, sketch, plane, ring):
     rows, frames = panel.shape
+    half = jax.ShapeDtypeStruct((plane, 2 * ring, K), jnp.float32)
     return pl.pallas_call(
         cross_kernel,
-        out_shape=jax.ShapeDtypeStruct((frames, K), jnp.float32),
-        grid=(rows // tile,),
-        in_specs=[
-            pl.BlockSpec((tile, frames), lambda i: (i, 0)),
-            pl.BlockSpec((tile, K), lambda i: (i, 0)),
+        out_shape=(half, half),
+        in_specs=[SMEM, HBM, HBM],
+        out_specs=(VMEM, VMEM),
+        scratch_shapes=[
+            pltpu.VMEM(panel.shape, jnp.float32),
+            pltpu.VMEM(sketch.shape, jnp.float32),
+            pltpu.VMEM((frames, K), jnp.float32),
+            pltpu.SemaphoreType.DMA((2, len(CROSS_STEPS))),
         ],
-        out_specs=pl.BlockSpec((frames, K), lambda i: (0, 0)),
         cost_estimate=pl.CostEstimate(
             flops=6 * rows * K * frames, bytes_accessed=8 * rows * K, transcendentals=0
         ),
-        compiler_params=pltpu.CompilerParams(vmem_limit_bytes=28 << 20),
+        compiler_params=pltpu.CompilerParams(vmem_limit_bytes=52 << 20),
         name="cross",
-    )(panel, sketch)
+    )(core, panel, sketch)
 
 
 def factor_block(t, bc_ref):
@@ -254,61 +285,71 @@
 
 
 def lower_inverse(core, mine, other):
-    vmem = pl.BlockSpec(memory_space=pltpu.VMEM)
     return pl.pallas_call(
         factor_kernel,
         out_shape=jax.ShapeDtypeStruct((K, K), jnp.float32),
-        in_specs=[pl.BlockSpec(memory_space=pltpu.SMEM), vmem, vmem],
-        out_specs=vmem,
+        in_specs=[SMEM, VMEM, VMEM],
+        out_specs=VMEM,
         scratch_shapes=[
             pltpu.VMEM((2, B, K + B), jnp.float32),
             pltpu.VMEM((K, K), jnp.float32),
             pltpu.VMEM((B // G, G + 1, G, B), jnp.float32),
         ],
         cost_estimate=pl.CostEstimate(flops=8_000_000_000, bytes_accessed=2_000_000, transcendentals=0),
-        compiler_params=pltpu.CompilerParams(vmem_limit_bytes=12 << 20),
+        compiler_params=pltpu.CompilerParams(vmem_limit_bytes=8 << 20),
         name="factor",
     )(core, mine, other)
 
 
-def basis_kernel(scale, x_ref, w_ref, c_ref, o_ref, q_ref, hi_ref, lo_ref):
+def basis_kernel(scale, x_hbm, w_ref, c_ref, o_hbm, q_ref, x_ref, o_ref, in_sems, out_sems):
+    loads = start_loads(((x_hbm, x_ref),), in_sems, BASIS_STEPS)
     h = K // 2
+    hi, lo = halves(w_ref[...])
+    wl = (hi[:h, :h], lo[:h, :h])
+    wr = (hi[h:, :], lo[h:, :])
 
     def times(rows):
-        rl, rr = halves(rows[:, :h]), halves(rows[:, h:])
-        wl = (hi_ref[:h, :h], lo_ref[:h, :h])
-        wr = (hi_ref[h:, :h], lo_ref[h:, :h]), (hi_ref[h:, h:], lo_ref[h:, h:])
-        return dot3(rl, wl, 1, 1), dot3(rl, wr[0], 1, 1) + dot3(rr, wr[1], 1, 1)
-
-    @pl.when(pl.program_id(0) == 0)
-    def _():
-        hi_ref[...], lo_ref[...] = halves(w_ref[...])
-        left, right = times(c_ref[...])
-        q_ref[:, :h] = left * scale
-        q_ref[:, h:] = right * scale
-
-    o_ref[:, :h], o_ref[:, h:] = times(x_ref[...])
-
-
-def apply_inverse(sketch, winv, crows, scale, tile=1024):
+        hi, lo = halves(rows)
+        return dot3((hi[:, :h], lo[:, :h]), wl, 1, 1), dot3((hi, lo), wr, 1, 1)
+
+    left, right = times(c_ref[...])
+    q_ref[:, :h] = left * scale
+    q_ref[:, h:] = right * scale
+    stores = []
+    start = 0
+    for i, size in enumerate(BASIS_STEPS):
+        loads[i][0].wait()
+        rows = slice(start, start + size)
+        o_ref[rows, :h], o_ref[rows, h:] = times(x_ref[rows, :])
+        at = pl.ds(start, size)
+        stores.append(pltpu.make_async_copy(o_ref.at[at], o_hbm.at[at], out_sems.at[i]))
+        stores[-1].start()
+        start += size
+    for store in stores:
+        store.wait()
+
+
+def apply_inverse(sketch, winv, crows, scale):
     rows = sketch.shape[0]
     n = crows.shape[0]
-    fixed = pl.BlockSpec((K, K), lambda i: (0, 0))
-    small = pl.BlockSpec((n, K), lambda i: (0, 0))
     return pl.pallas_call(
         functools.partial(basis_kernel, scale),
         out_shape=(
             jax.ShapeDtypeStruct((rows, K), jnp.float32),
             jax.ShapeDtypeStruct((n, K), jnp.float32),
         ),
-        grid=(rows // tile,),
-        in_specs=[pl.BlockSpec((tile, K), lambda i: (i, 0)), fixed, small],
-        out_specs=(pl.BlockSpec((tile, K), lambda i: (i, 0)), small),
-        scratch_shapes=[pltpu.VMEM((K, K), jnp.bfloat16)] * 2,
+        in_specs=[HBM, VMEM, VMEM],
+        out_specs=(HBM, VMEM),
+        scratch_shapes=[
+            pltpu.VMEM((rows, K), jnp.float32),
+            pltpu.VMEM((rows, K), jnp.float32),
+            pltpu.SemaphoreType.DMA((1, len(BASIS_STEPS))),
+            pltpu.SemaphoreType.DMA((len(BASIS_STEPS),)),
+        ],
         cost_estimate=pl.CostEstimate(
             flops=6 * rows * K * K, bytes_accessed=8 * rows * K, transcendentals=0
         ),
-        compiler_params=pltpu.CompilerParams(vmem_limit_bytes=24 << 20),
+        compiler_params=pltpu.CompilerParams(vmem_limit_bytes=50 << 20),
         name="basis",
     )(sketch, winv, crows)
 
@@ -346,13 +387,9 @@
     other = lax.ppermute(mine, "c", SWAP)
     winv = lower_inverse(core.reshape(1), mine, other)
 
-    cross = cross_product(panel, sketch)
-    frames = cross.shape[0] // (ring * plane * 2)
-    cross = cross.reshape(ring, plane, 2, frames, K)
-    ckeep = lax.dynamic_index_in_dim(cross, core, 2, keepdims=False)
-    csend = lax.dynamic_index_in_dim(cross, 1 - core, 2, keepdims=False)
+    frames = panel.shape[1] // (ring * plane * 2)
+    ckeep, csend = cross_product(core.reshape(1), panel, sketch, plane, ring)
     chalf = ckeep + lax.ppermute(csend, "c", SWAP)
-    chalf = chalf.transpose(1, 0, 2, 3).reshape(plane, ring * frames, K)
     got = lax.all_to_all(chalf, PLANE, 0, 0, tiled=True)
     crows = jnp.sum(got, axis=0).reshape(ring, frames, K)
     got = lax.all_to_all(crows, "z", 0, 0, tiled=True)

time: 103 us -> 106 us (1.029)
  blocking collectives: 11.7 us -> 26.6 us
  starting transfers between devices: 29.5 us -> 19.6 us
  local copies, waits for them, and re-layouts: 9.51 us -> 0.77 us
  Pallas kernels: 24.7 us -> 32.3 us
    all_to_all x0 -> x1, blocking collectives: none -> 15.6 us  [on_device(): lax.all_to_all(half.reshape(plane, B // plane, K + B), PLANE, 0, 0, tiled...]
    all_to_all x1 -> x0, starting transfers between devices: 7.48 us -> none  [on_device(): lax.all_to_all(half.reshape(plane, B // plane, K + B), PLANE, 0, 0, tiled...]
    unnamed x8 -> x0, local copies, waits for them, and re-layouts: 6.56 us -> none
    pallas_call x2, Pallas kernels: 6.95 us -> 11.2 us  [the longest x1 5.79 us: cross_product(): pl.pallas_call(cross_kernel, out_shape=(half, half), in_specs=[SMEM, HBM,...]
    pallas_call x1, Pallas kernels: 4.71 us -> 8.07 us  [apply_inverse(): pl.pallas_call(functools.partial(basis_kernel, scale), out_shape=(jax.Sha...]
    ppermute x4, waiting for transfers between devices: 8.07 us -> 4.99 us  [shift(): return lax.ppermute(x, 'z', [(i, (i + by) % n) for i in range(n)])]
    all_to_all x1, starting transfers between devices: 7.23 us -> 4.79 us  [on_device(): lax.all_to_all(jnp.broadcast_to(part, (plane,) + part.shape), PLANE, 0, 0...]
    reshape x2 -> x0, local copies, waits for them, and re-layouts: 1.72 us -> none  [the longest x1 1.1 us: on_device(): chalf = chalf.transpose(1, 0, 2, 3).reshape(plane, ring * frames, K)]
  transfers between devices with their start and end apart: 10 -> 9, of which waited for: 7 -> 5; matrix products, arithmetic and copies ran while one was open for 3% -> 2% of each run, Pallas kernels for 4% -> 5%
where the time goes in v1:
time: 106 us
  Pallas kernels  32.3 us (30%)
  blocking collectives  26.6 us (25%)
  waiting for transfers between devices  24.8 us (23%)
  starting transfers between devices  19.6 us (18%)
    all_to_all x1, blocking collectives, on_device(): lax.all_to_all(half.reshape(plane, B // plane, K + B), PLANE, 0, 0, tiled...  15.6 us
    pallas_call x1, Pallas kernels, lower_inverse(): pl.pallas_call(factor_kernel, out_shape=jax.ShapeDtypeStruct((K, K), jnp....  13.1 us
    all_to_all x1, blocking collectives, on_device(): got = lax.all_to_all(crows, 'z', 0, 0, tiled=True)  11 us
    all_to_all x1, waiting for transfers between devices, on_device(): got = lax.all_to_all(chalf, PLANE, 0, 0, tiled=True)  10 us
    ppermute x4, starting transfers between devices, shift(): return lax.ppermute(x, 'z', [(i, (i + by) % n) for i in range(n)])  9.76 us
    all_to_all x1, waiting for transfers between devices, on_device(): lax.all_to_all(jnp.broadcast_to(part, (plane,) + part.shape), PLANE, 0, 0...  8.14 us
    pallas_call x1, Pallas kernels, apply_inverse(): pl.pallas_call(functools.partial(basis_kernel, scale), out_shape=(jax.Sha...  8.07 us
    pallas_call x1, Pallas kernels, cross_product(): pl.pallas_call(cross_kernel, out_shape=(half, half), in_specs=[SMEM, HBM,...  5.79 us
  transfers between devices with their start and end apart: 9, of which 5 were waited for; matrix products, arithmetic and copies ran while one was open for 2% of the time, Pallas kernels for 5%

profile of v1, /device:TPU:2, one launch (start us, length us, event | category | flops | bytes accessed | tf_op | source)
XLA Modules:
  0.0 105.9 jit_solution(6736682615367179802)
XLA Ops:
  0.6 5.4 %gram.1 = (f32[128,640]{1,0:T(8,128)S(1)}, f32[128,640]{1,0:T(8,128)S(1)}) custom-call(s32[1]{0:T(128)} %bitcast.core_ref, f32[2048,512]{1,0:T(8,128)} %x_hbm.5), custom_call_target="tpu_custom_call" | custom-call | flops 3221225472 | bytes 4194304 | tf_op jit(solution)/shard_map/gram/pallas_call | solution.py:111
  6.0 0.1 collective-permute-start
  6.1 1.6 %collective-permute-done = f32[128,640]{1,0:T(8,128)S(1)} collective-permute-done((f32[128,640]{1,0:T(8,128)S(1)}, f32[128,640]{1,0:T(8,128)S(1)}, u32[]{:S(2)}, u32[]{:S(2)}) %collective-permute-start) | collective-permute-done | bytes 327712 | tf_op jit(solution)/shard_map/ppermute | solution.py:381
  7.8 15.6 %all_to_all.20 = f32[16,8,640]{2,1,0:T(8,128)S(1)} all-to-all(f32[16,8,640]{2,1,0:T(8,128)S(1)} %add_bitcast_fusion), channel_id=1, replica_groups=mesh['z'=8,'y'=4,'x'=4,'c'=2] {'y','x'}, dimensions={0} | all-to-all | bytes 655360 | tf_op jit(solution)/shard_map/all_to_all | solution.py:382
  23.4 5.9 %collective-permute-start.2 = (f32[8,640]{1,0:T(8,128)S(1)}, f32[8,640]{1,0:T(8,128)S(1)}, u32[]{:S(2)}, u32[]{:S(2)}) collective-permute-start(f32[8,640]{1,0:T(8,128)S(1)} %reduce_sum.27), channel_id=1, source_target_pairs={{0,224},{32,0},{64,32},{96,64},{128,96},{160,128},{192,160},{224,1... | collective-permute-start | bytes 61448 | tf_op jit(solution)/shard_map/ppermute | solution.py:362
  29.3 0.0 collective-permute-start.1
  29.3 1.5 %collective-permute-done.2 = f32[8,640]{1,0:T(8,128)S(1)} collective-permute-done((f32[8,640]{1,0:T(8,128)S(1)}, f32[8,640]{1,0:T(8,128)S(1)}, u32[]{:S(2)}, u32[]{:S(2)}) %collective-permute-start.2) | collective-permute-done | bytes 20512 | tf_op jit(solution)/shard_map/ppermute | solution.py:362
  30.8 3.5 %collective-permute-done.1 = f32[8,640]{1,0:T(8,128)S(1)} collective-permute-done((f32[8,640]{1,0:T(8,128)S(1)}, f32[8,640]{1,0:T(8,128)S(1)}, u32[]{:S(2)}, u32[]{:S(2)}) %collective-permute-start.1) | collective-permute-done | bytes 20512 | tf_op jit(solution)/shard_map/ppermute | solution.py:362
  34.3 0.7 collective-permute-start.4
  35.0 3.1 %collective-permute-start.3 = (f32[8,640]{1,0:T(8,128)S(1)}, f32[8,640]{1,0:T(8,128)S(1)}, u32[]{:S(2)}, u32[]{:S(2)}) collective-permute-start(f32[8,640]{1,0:T(8,128)S(1)} %get-tuple-element.10), channel_id=1, source_target_pairs={{0,96},{32,128},{64,160},{96,192},{128,224},{160,0},{192,32},{224,... | collective-permute-start | bytes 61448 | tf_op jit(solution)/shard_map/ppermute | solution.py:362
  38.2 5.8 %cross.1 = (f32[16,16,512]{2,1,0:T(8,128)S(1)}, f32[16,16,512]{2,1,0:T(8,128)S(1)}) custom-call(s32[1]{0:T(128)} %bitcast.core_ref, f32[2048,512]{1,0:T(8,128)} %p_hbm.1, f32[2048,512]{1,0:T(8,128)} %x_hbm.5), custom_call_target="tpu_custom_call" | custom-call | flops 3221225472 | bytes 8388608 | tf_op jit(solution)/shard_map/cross/pallas_call | solution.py:157
  44.0 0.1 collective-permute-start.6
  44.1 0.0 collective-permute-done.4
  44.1 0.0 collective-permute-done.3
  44.1 0.7 broadcast_in_dim.3
  44.9 4.8 %all-to-all-start.1 = ((f32[16,8,640]{2,1,0:T(8,128)}), f32[16,8,640]{2,1,0:T(8,128)S(1)}, u32[]{:S(2)}, u32[]{:S(2)}) async-start(f32[16,8,640]{2,1,0:T(8,128)} %broadcast_in_dim.3), calls=%async_computation.1 | async-start | bytes 655360 | tf_op jit(solution)/shard_map/all_to_all | solution.py:384
  49.6 0.9 add.23
  50.5 8.1 %all-to-all-done.1 = f32[16,8,640]{2,1,0:T(8,128)S(1)} async-done(((f32[16,8,640]{2,1,0:T(8,128)}), f32[16,8,640]{2,1,0:T(8,128)S(1)}, u32[]{:S(2)}, u32[]{:S(2)}) %all-to-all-start.1) | async-done | bytes 327712 | tf_op jit(solution)/shard_map/all_to_all | solution.py:384
  58.7 4.8 %all-to-all-start.2 = ((f32[16,16,512]{2,1,0:T(8,128)}), f32[16,16,512]{2,1,0:T(8,128)S(1)}, u32[]{:S(2)}, u32[]{:S(2)}) async-start(f32[16,16,512]{2,1,0:T(8,128)} %add.23), calls=%async_computation.2 | async-start | bytes 1048576 | tf_op jit(solution)/shard_map/all_to_all | solution.py:393
  63.5 0.0 collective-permute-start.5
  63.5 10.0 %all-to-all-done.2 = f32[16,16,512]{2,1,0:T(8,128)S(1)} async-done(((f32[16,16,512]{2,1,0:T(8,128)}), f32[16,16,512]{2,1,0:T(8,128)S(1)}, u32[]{:S(2)}, u32[]{:S(2)}) %all-to-all-start.2) | async-done | bytes 524320 | tf_op jit(solution)/shard_map/all_to_all | solution.py:393
  73.6 11.0 %all_to_all.21 = f32[8,2,512]{2,1,0:T(2,128)S(1)} all-to-all(f32[8,2,512]{2,1,0:T(2,128)S(1)} %reshape.21), channel_id=1, replica_groups=mesh['z'=8,'y'=4,'x'=4,'c'=2] {'z'}, dimensions={0} | all-to-all | bytes 65536 | tf_op jit(solution)/shard_map/all_to_all | solution.py:395
  84.6 13.1 %factor.1.w_ref = f32[512,512]{1,0:T(8,128)S(1)} custom-call(s32[1]{0:T(128)} %bitcast.core_ref, f32[128,640]{1,0:T(8,128)S(1)} %bitcast.5, f32[128,640]{1,0:T(8,128)S(1)} %collective-permute-done.5.other_ref), custom_call_target="tpu_custom_call" | custom-call | flops 8000000000 | bytes 2000000 | tf_op jit(solution)/shard_map/factor/pallas_call | solution.py:288
  97.7 8.1 %basis.1 = (f32[2048,512]{1,0:T(8,128)}, f32[2,512]{1,0:T(2,128)}) custom-call(f32[2048,512]{1,0:T(8,128)} %x_hbm.5, f32[512,512]{1,0:T(8,128)S(1)} %factor.1.w_ref, f32[2,512]{1,0:T(2,128)S(1)} %reduce_sum.29.c_ref), custom_call_target="tpu_custom_call" | custom-call | flops 3221225472 | bytes 8388608 | tf_op jit(solution)/shard_map/basis/pallas_call | solution.py:335
  (9 shorter events, 0.2 us)
Async XLA Ops:
  6.0 1.7 %collective-permute-start = (f32[128,640]{1,0:T(8,128)S(1)}, f32[128,640]{1,0:T(8,128)S(1)}, u32[]{:S(2)}, u32[]{:S(2)}) collective-permute-start(f32[128,640]{1,0:T(8,128)S(1)} %get-tuple-element.7), channel_id=1, source_target_pairs={{0,1},{1,0},{2,3},{3,2},{4,5},{5,4},{6,7},{7,6},{8,9},{9,8},{10,11... | collective-permute-start | bytes 983048 | tf_op jit(solution)/shard_map/ppermute | solution.py:381
  23.4 7.4 %collective-permute-start.2 = (f32[8,640]{1,0:T(8,128)S(1)}, f32[8,640]{1,0:T(8,128)S(1)}, u32[]{:S(2)}, u32[]{:S(2)}) collective-permute-start(f32[8,640]{1,0:T(8,128)S(1)} %reduce_sum.27), channel_id=1, source_target_pairs={{0,224},{32,0},{64,32},{96,64},{128,96},{160,128},{192,160},{224,1... | collective-permute-start | bytes 61448 | tf_op jit(solution)/shard_map/ppermute | solution.py:362
  29.3 5.0 %collective-permute-start.1 = (f32[8,640]{1,0:T(8,128)S(1)}, f32[8,640]{1,0:T(8,128)S(1)}, u32[]{:S(2)}, u32[]{:S(2)}) collective-permute-start(f32[8,640]{1,0:T(8,128)S(1)} %reduce_sum.27), channel_id=1, source_target_pairs={{0,32},{32,64},{64,96},{96,128},{128,160},{160,192},{192,224},{224... | collective-permute-start | bytes 61448 | tf_op jit(solution)/shard_map/ppermute | solution.py:362
  34.3 9.7 %collective-permute-start.4 = (f32[8,640]{1,0:T(8,128)S(1)}, f32[8,640]{1,0:T(8,128)S(1)}, u32[]{:S(2)}, u32[]{:S(2)}) collective-permute-start(f32[8,640]{1,0:T(8,128)S(1)} %get-tuple-element.11), channel_id=1, source_target_pairs={{0,160},{32,192},{64,224},{96,0},{128,32},{160,64},{192,96},{224,1... | collective-permute-start | bytes 61448 | tf_op jit(solution)/shard_map/ppermute | solution.py:362
  35.0 9.1 %collective-permute-start.3 = (f32[8,640]{1,0:T(8,128)S(1)}, f32[8,640]{1,0:T(8,128)S(1)}, u32[]{:S(2)}, u32[]{:S(2)}) collective-permute-start(f32[8,640]{1,0:T(8,128)S(1)} %get-tuple-element.10), channel_id=1, source_target_pairs={{0,96},{32,128},{64,160},{96,192},{128,224},{160,0},{192,32},{224,... | collective-permute-start | bytes 61448 | tf_op jit(solution)/shard_map/ppermute | solution.py:362
  44.0 5.7 %collective-permute-start.6 = (f32[16,16,512]{2,1,0:T(8,128)S(1)}, f32[16,16,512]{2,1,0:T(8,128)S(1)}, u32[]{:S(2)}, u32[]{:S(2)}) collective-permute-start(f32[16,16,512]{2,1,0:T(8,128)S(1)} %get-tuple-element.9), channel_id=1, source_target_pairs={{0,1},{1,0},{2,3},{3,2},{4,5},{5,4},{6,7},{7,6},{8,9},{9,8},{10,11... | collective-permute-start | bytes 1572872 | tf_op jit(solution)/shard_map/ppermute | solution.py:392
  44.9 13.8 %all-to-all-start.1 = ((f32[16,8,640]{2,1,0:T(8,128)}), f32[16,8,640]{2,1,0:T(8,128)S(1)}, u32[]{:S(2)}, u32[]{:S(2)}) async-start(f32[16,8,640]{2,1,0:T(8,128)} %broadcast_in_dim.3), calls=%async_computation.1 | async-start | bytes 655360 | tf_op jit(solution)/shard_map/all_to_all | solution.py:384
  58.7 14.8 %all-to-all-start.2 = ((f32[16,16,512]{2,1,0:T(8,128)}), f32[16,16,512]{2,1,0:T(8,128)S(1)}, u32[]{:S(2)}, u32[]{:S(2)}) async-start(f32[16,16,512]{2,1,0:T(8,128)} %add.23), calls=%async_computation.2 | async-start | bytes 1048576 | tf_op jit(solution)/shard_map/all_to_all | solution.py:393
  63.5 21.1 %collective-permute-start.5 = (f32[128,640]{1,0:T(8,128)S(1)}, f32[128,640]{1,0:T(8,128)S(1)}, u32[]{:S(2)}, u32[]{:S(2)}) collective-permute-start(f32[128,640]{1,0:T(8,128)S(1)} %bitcast.4), channel_id=1, source_target_pairs={{0,1},{1,0},{2,3},{3,2},{4,5},{5,4},{6,7},{7,6},{8,9},{9,8},{10,11... | collective-permute-start | bytes 983048 | tf_op jit(solution)/shard_map/ppermute | solution.py:387
